TPU v7x, 512 devices: a whole 4x4x16 slice. The times are simulated.
512 devices in a mesh: gx: 16 (over z_hi, y, core), gy: 4 (over x), gz: 8 (over z_lo).
Axes of the slice: x: 4, y: 4, z: 16 (z_hi: 2, z_lo: 8; z = z_hi * 8 + z_lo), core: 2. Of those that a mesh axis runs over, the one named last changes fastest.
Arguments:
- body_load: float32 [32, 16, 64, 192], P('gx', 'gy', 'gz'), may hold values from -6 to 6
- probe_load: float32 [32, 16, 64, 192], P('gx', 'gy', 'gz'), may hold values from -6 to 6
- density: float32 [32, 16, 64], P('gx', 'gy', 'gz'), may hold values from 0.3 to 1
- link_types: int32 [32, 16, 64, 7], P('gx', 'gy', 'gz'), may hold values from 0 to 4, as said below
- off_blocks: bfloat16 [4, 192, 192], replicated, may hold values from -0.4375 to 0.4375
- self_blocks: bfloat16 [4, 192, 192], replicated, as said below
- block_owner: int32 [32, 16, 64], P('gx', 'gy', 'gz'), may hold values from 0 to 4095, as said below
Outputs:
- state_field: float32 [32, 16, 64, 192], P('gx', 'gy', 'gz')
- adjoint_field: float32 [32, 16, 64, 192], P('gx', 'gy', 'gz')
- coarse_sensitivity: float32 [4096], P(('gx', 'gy', 'gz'))
Inputs may be any that keep to these rules, and one draw needn't show every extreme that they name: `link_types`: entries 0, 1, 2 of a group name the kind of its coupling to the next group along the first, second and third dimension (4: no coupling, always so on the grid's last layer); entry 3 + k equals entry k of the group one step lower along dimension k (4 on the first layer); entry 6 names the kind of the group's own block and is below 4. `block_owner`: every design block is named by exactly 8 node groups. `self_blocks`: each own block is symmetric and its diagonal entries exceed 3.8.
All inputs are finite; a program needn't handle non-finite values.
Results may differ from a plain program's by a relative error of at most 0.0012.
Values may be sent and summed in bfloat16 or wider, within the bound.
A program may use at most 64 MiB of HBM per device.

v0:
```python
import jax
import jax.numpy as jnp
from jax import lax
from jax.sharding import PartitionSpec as P

ITERS = 4
GPB = 8


def with_halo(array, sides, width):
    for axis, dim in sides:
        peers, length = (lax.axis_size(axis), array.shape[dim])
        up = [(i, (i + 1) % peers) for i in range(peers - 1)]
        down = [(j, i) for i, j in up]
        last = lax.slice_in_dim(array, length - width, length, axis=dim)
        initial = lax.slice_in_dim(array, 0, width, axis=dim)
        before = lax.ppermute(last, axis, up)
        after = lax.ppermute(initial, axis, down)
        array = jnp.concatenate([before, array, after], axis=dim)
    return array


def level_masks(type_codes, level_count):
    levels = lax.broadcasted_iota(jnp.int32, type_codes.shape + (level_count,), 3)
    return (type_codes[..., None] == levels).astype(jnp.bfloat16)


def typed_product(window, selector, block_table):
    spread = window[:, :, :, :, None, :] * selector[None, :, :, :, :, None]
    flattened = spread.reshape(-1, block_table.shape[0])
    return jnp.dot(flattened, block_table, preferred_element_type=jnp.float32).reshape(window.shape)


def cut_window(padded, shift):
    span_x = padded.shape[1] - 2
    span_y = padded.shape[2] - 2
    span_z = padded.shape[3] - 2
    return padded[
        :,
        1 + shift[0] : 1 + shift[0] + span_x,
        1 + shift[1] : 1 + shift[1] + span_y,
        1 + shift[2] : 1 + shift[2] + span_z,
        :,
    ]


def local_image(padded, selectors, tables, stiff_scale):
    up_table, low_table, own_table = tables
    accumulated = typed_product(cut_window(padded, (0, 0, 0)), selectors[6], own_table)
    offsets = ((1, 0, 0), (0, 1, 0), (0, 0, 1))
    for k in range(3):
        upper = offsets[k]
        lower = (-upper[0], -upper[1], -upper[2])
        accumulated = accumulated + typed_product(cut_window(padded, upper), selectors[k], up_table)
        accumulated = accumulated + typed_product(
            cut_window(padded, lower), selectors[3 + k], low_table
        )
    return accumulated * stiff_scale[None, :, :, :, None]


def local(body_load, probe_load, density, link_types, off_blocks, self_blocks, block_owner):
    dof_count = body_load.shape[-1]
    type_count = off_blocks.shape[0]
    self_count = self_blocks.shape[0]
    stiff_scale = density**1.5
    selectors = [level_masks(link_types[..., j], type_count) for j in range(6)]
    selectors.append(level_masks(link_types[..., 6], self_count))
    up_table = jnp.swapaxes(off_blocks, 1, 2).reshape(type_count * dof_count, dof_count)
    low_table = off_blocks.reshape(type_count * dof_count, dof_count)
    own_table = self_blocks.reshape(self_count * dof_count, dof_count)
    tables = (up_table, low_table, own_table)
    diagonals = jnp.diagonal(self_blocks, axis1=1, axis2=2).astype(jnp.float32)
    pivots = jnp.zeros(body_load.shape, jnp.float32)
    for level in range(self_count):
        pivots = (
            pivots + selectors[6][..., level : level + 1].astype(jnp.float32) * diagonals[level]
        )
    targets = jnp.stack([body_load, probe_load])
    residual = targets
    solution = jnp.zeros_like(targets)
    for sweep in range(ITERS):
        precond = residual / pivots[None]
        shipped = (precond * stiff_scale[None, :, :, :, None]).astype(jnp.bfloat16)
        padded = with_halo(shipped, (("gx", 1), ("gy", 2), ("gz", 3)), 1)
        image_field = local_image(padded, selectors, tables, stiff_scale)
        projected = jnp.sum(residual * image_field, axis=(1, 2, 3, 4))
        energy = jnp.sum(image_field * image_field, axis=(1, 2, 3, 4))
        projected, energy = lax.psum((projected, energy), ("gx", "gy", "gz"))
        step_size = projected / (energy + 1e-06)
        solution = solution + step_size[:, None, None, None, None] * precond
        residual = residual - step_size[:, None, None, None, None] * image_field
    applied = targets - residual
    bracket = jnp.sum(solution[1] * applied[0] + solution[0] * applied[1], axis=-1)
    sensitivity = -1.5 * bracket / density
    weighted = density * sensitivity
    groups_here = density.shape[0] * density.shape[1] * density.shape[2]
    blocks_here = groups_here // GPB
    size_x = lax.axis_size("gx")
    size_y = lax.axis_size("gy")
    size_z = lax.axis_size("gz")
    block_total = blocks_here * size_x * size_y * size_z
    owners = block_owner.reshape(-1)
    numerator = jnp.zeros((block_total,), jnp.float32).at[owners].add(weighted.reshape(-1))
    denominator = jnp.zeros((block_total,), jnp.float32).at[owners].add(density.reshape(-1))
    numerator, denominator = (
        lax.psum_scatter(numerator, ("gx", "gy", "gz"), scatter_dimension=0, tiled=True),
        lax.psum_scatter(denominator, ("gx", "gy", "gz"), scatter_dimension=0, tiled=True),
    )
    return (solution[0], solution[1], numerator / denominator)


def solution(mesh):
    in_specs = (
        P("gx", "gy", "gz", None),
        P("gx", "gy", "gz", None),
        P("gx", "gy", "gz"),
        P("gx", "gy", "gz", None),
        P(),
        P(),
        P("gx", "gy", "gz"),
    )
    out_specs = (P("gx", "gy", "gz", None), P("gx", "gy", "gz", None), P(("gx", "gy", "gz")))
    return jax.shard_map(local, mesh=mesh, in_specs=in_specs, out_specs=out_specs, check_vma=False)
```

profile of v0, /device:TPU:1, one launch (start us, length us, event | category | flops | bytes accessed | tf_op | source)
XLA Modules:
  0.0 689.2 jit_solution(9838900810073035173)
XLA Ops:
  1.5 7.8 %copy.38 = bf16[4,192,192]{0,2,1:T(8,128)(2,1)} copy(bf16[4,192,192]{2,1,0:T(8,128)(2,1)} %param.12) | data formatting | bytes 589824 | tf_op args[5]
  9.3 5.3 gather_fusion
  15.2 8.8 %collective-permute-start = (bf16[2,1,4,8,192]{4,3,2,1,0:T(8,128)(2,1)S(1)}, bf16[2,1,4,8,192]{4,3,2,1,0:T(8,128)(2,1)S(1)}, u32[]{:S(2)}, u32[]{:S(2)}) collective-permute-start(bf16[2,1,4,8,192]{4,3,2,1,0:T(8,128)(2,1)S(1)} %get-tuple-element.83), channel_id=1, source_target_pairs={{32,0},{64,32},{96,64},{128,96},{160,128},{192,160},{224,192},{256... | collective-permute-start | bytes 73736 | tf_op jit(solution)/shard_map/ppermute | solution.py:18
  24.0 1.9 collective-permute-start.1
  28.5 4.0 collective-permute-start.3
  34.8 4.0 collective-permute-start.5
  41.4 125.0 %all-reduce.6 = (f32[2]{0:T(128)S(1)}, f32[2]{0:T(128)S(1)}) all-reduce(f32[2]{0:T(128)S(1)} %get-tuple-element.10, f32[2]{0:T(128)S(1)} %get-tuple-element.9), channel_id=1, replica_groups=mesh['gx'=16,'gy'=4,'gz'=8] {'gx','gy','gz'}, use_global_device_ids=true, to_apply=%region_1.2 | all-reduce | flops 4 | bytes 32 | tf_op jit(solution)/shard_map/psum | solution.py:88
  166.6 2.9 collective-permute-start.6
  169.5 2.7 collective-permute-start.7
  174.5 4.0 collective-permute-start.9
  180.9 4.0 collective-permute-start.11
  187.5 117.6 %all-reduce.5 = (f32[2]{0:T(128)S(1)}, f32[2]{0:T(128)S(1)}) all-reduce(f32[2]{0:T(128)S(1)} %get-tuple-element.8, f32[2]{0:T(128)S(1)} %get-tuple-element.7), channel_id=1, replica_groups=mesh['gx'=16,'gy'=4,'gz'=8] {'gx','gy','gz'}, use_global_device_ids=true, to_apply=%region_5.6 | all-reduce | flops 4 | bytes 32 | tf_op jit(solution)/shard_map/psum | solution.py:88
  305.2 2.6 collective-permute-start.12
  307.8 3.0 collective-permute-start.13
  311.8 1.3 collective-permute-start.14
  313.1 4.0 collective-permute-start.15
  319.6 4.0 collective-permute-start.17
  326.2 120.1 %all-reduce.4 = (f32[2]{0:T(128)S(1)}, f32[2]{0:T(128)S(1)}) all-reduce(f32[2]{0:T(128)S(1)} %get-tuple-element.6, f32[2]{0:T(128)S(1)} %get-tuple-element.5), channel_id=1, replica_groups=mesh['gx'=16,'gy'=4,'gz'=8] {'gx','gy','gz'}, use_global_device_ids=true, to_apply=%region_9.10 | all-reduce | flops 4 | bytes 32 | tf_op jit(solution)/shard_map/psum | solution.py:88
  446.4 3.1 collective-permute-start.18
  449.6 2.5 collective-permute-start.19
  454.6 4.0 collective-permute-start.21
  461.0 4.0 collective-permute-start.23
  467.6 118.0 %all-reduce.3 = (f32[2]{0:T(128)S(1)}, f32[2]{0:T(128)S(1)}) all-reduce(f32[2]{0:T(128)S(1)} %get-tuple-element.4, f32[2]{0:T(128)S(1)} %get-tuple-element.3), channel_id=1, replica_groups=mesh['gx'=16,'gy'=4,'gz'=8] {'gx','gy','gz'}, use_global_device_ids=true, to_apply=%region_13.14 | all-reduce | flops 4 | bytes 32 | tf_op jit(solution)/shard_map/psum | solution.py:88
  587.4 101.2 %all-reduce.2 = (f32[4096]{0:T(1024)S(1)}, f32[4096]{0:T(1024)S(1)}) all-reduce(f32[4096]{0:T(1024)S(1)} %scatter_custom_fusion.1, f32[4096]{0:T(1024)S(1)} %scatter_custom_fusion), channel_id=3, replica_groups=mesh['gx'=16,'gy'=4,'gz'=8] {'gx','gy','gz'}, use_global_device_ids=true, to_apply=%region_20.21.clone | all-reduce | flops 8192 | bytes 65536
  (123 shorter events, 32.1 us)
Async XLA Ops:
  15.2 10.8 %collective-permute-start = (bf16[2,1,4,8,192]{4,3,2,1,0:T(8,128)(2,1)S(1)}, bf16[2,1,4,8,192]{4,3,2,1,0:T(8,128)(2,1)S(1)}, u32[]{:S(2)}, u32[]{:S(2)}) collective-permute-start(bf16[2,1,4,8,192]{4,3,2,1,0:T(8,128)(2,1)S(1)} %get-tuple-element.83), channel_id=1, source_target_pairs={{32,0},{64,32},{96,64},{128,96},{160,128},{192,160},{224,192},{256... | collective-permute-start | bytes 73736 | tf_op jit(solution)/shard_map/ppermute | solution.py:18
  24.0 3.1 collective-permute-start.1
  27.2 5.6 collective-permute-start.2
  28.5 5.0 collective-permute-start.3
  33.5 6.0 collective-permute-start.4
  34.8 5.2 collective-permute-start.5
  166.6 5.6 collective-permute-start.6
  169.5 3.7 collective-permute-start.7
  173.2 5.6 collective-permute-start.8
  174.5 5.0 collective-permute-start.9
  179.6 6.0 collective-permute-start.10
  180.9 5.2 collective-permute-start.11
  305.2 5.7 collective-permute-start.12
  307.8 4.0 collective-permute-start.13
  311.8 5.6 collective-permute-start.14
  313.1 5.2 collective-permute-start.15
  318.3 6.0 collective-permute-start.16
  319.6 5.2 collective-permute-start.17
  446.4 6.8 collective-permute-start.18
  449.6 3.7 collective-permute-start.19
  453.3 5.6 collective-permute-start.20
  454.6 5.0 collective-permute-start.21
  459.7 6.0 collective-permute-start.22
  461.0 5.2 collective-permute-start.23
  (7 other events, 651.9 us)
where the time goes:
time: 691 us; the launch traced here: 689 us
  blocking collectives  582 us (84%)
  starting transfers between devices  69.6 us (10%)
  local copies, waits for them, and re-layouts  14.6 us (2%)
  matrix products  9.27 us (1%)
  waiting for transfers between devices  7.56 us (1%)
    psum x4, blocking collectives, local(): projected, energy = lax.psum((projected, energy), ('gx', 'gy', 'gz'))  481 us
    unnamed x1, blocking collectives  101 us
    ppermute x12, starting transfers between devices, with_halo(): before = lax.ppermute(last, axis, up)  41.9 us
    ppermute x12, starting transfers between devices, with_halo(): after = lax.ppermute(initial, axis, down)  27.7 us
  transfers between devices with their start and end apart: 24, of which 11 were waited for; matrix products, arithmetic and copies ran while one was open for 1% of the time, Pallas kernels for 0%

commit v1 on v0

--- a/solution.py
+++ b/solution.py
@@ -85,7 +85,7 @@
         image_field = local_image(padded, selectors, tables, stiff_scale)
         projected = jnp.sum(residual * image_field, axis=(1, 2, 3, 4))
         energy = jnp.sum(image_field * image_field, axis=(1, 2, 3, 4))
-        projected, energy = lax.psum((projected, energy), ("gx", "gy", "gz"))
+        projected, energy = lax.psum(lax.psum((projected, energy), ("gy", "gz")), "gx")
         step_size = projected / (energy + 1e-06)
         solution = solution + step_size[:, None, None, None, None] * precond
         residual = residual - step_size[:, None, None, None, None] * image_field

time: 691 us -> 985 us (1.43)
  blocking collectives: 582 us -> 867 us
    psum x4 -> x8, blocking collectives: 481 us -> 730 us  [the longest x4 414 us: local(): lax.psum((projected, energy), ('gy', 'gz'))]
    unnamed x1, blocking collectives: 101 us -> 137 us
    ppermute x12, starting transfers between devices: 41.9 us -> 52.9 us  [with_halo(): before = lax.ppermute(last, axis, up)]
where the time goes in v1:
time: 985 us; the launch traced here: 983 us
  blocking collectives  867 us (88%)
  starting transfers between devices  79.2 us (8%)
  local copies, waits for them, and re-layouts  14.6 us (1%)
    psum x4, blocking collectives, local(): lax.psum((projected, energy), ('gy', 'gz'))  414 us
    psum x4, blocking collectives, local(): lax.psum(lax.psum((projected, energy), ('gy', 'gz')), 'gx')  316 us
    unnamed x1, blocking collectives  137 us
    ppermute x12, starting transfers between devices, with_halo(): before = lax.ppermute(last, axis, up)  52.9 us
    ppermute x12, starting transfers between devices, with_halo(): after = lax.ppermute(initial, axis, down)  26.3 us
  transfers between devices with their start and end apart: 24, of which 11 were waited for; matrix products, arithmetic and copies ran while one was open for 1% of the time, Pallas kernels for 0%

profile of v1, /device:TPU:1, one launch (start us, length us, event | category | flops | bytes accessed | tf_op | source)
XLA Modules:
  0.0 983.5 jit_solution(1623971702019658521)
XLA Ops:
  1.5 7.8 copy.38
  9.3 5.4 gather_fusion
  15.3 8.8 collective-permute-start
  28.5 4.0 collective-permute-start.3
  34.9 4.0 collective-permute-start.5
  41.5 109.4 %all-reduce.6 = (f32[2]{0:T(128)S(1)}, f32[2]{0:T(128)S(1)}) all-reduce(f32[2]{0:T(128)S(1)} %get-tuple-element.10, f32[2]{0:T(128)S(1)} %get-tuple-element.9), channel_id=1, replica_groups=mesh['gx'=16,'gy'=4,'gz'=8] {'gy','gz'}, use_global_device_ids=true, to_apply=%region_1.2 | all-reduce | flops 4 | bytes 32 | tf_op jit(solution)/shard_map/psum | solution.py:88
  150.9 77.4 %all-reduce.10 = (f32[2]{0:T(128)S(1)}, f32[2]{0:T(128)S(1)}) all-reduce(f32[2]{0:T(128)S(1)} %get-tuple-element.23, f32[2]{0:T(128)S(1)} %get-tuple-element.24), channel_id=1, replica_groups=mesh['gx'=16,'gy'=4,'gz'=8] {'gx'}, use_global_device_ids=true, to_apply=%region_2.3 | all-reduce | flops 4 | bytes 32 | tf_op jit(solution)/shard_map/psum | solution.py:88
  228.4 2.6 collective-permute-start.6
  230.9 3.0 collective-permute-start.7
  236.3 4.0 collective-permute-start.9
  242.8 4.0 collective-permute-start.11
  249.5 101.3 %all-reduce.5 = (f32[2]{0:T(128)S(1)}, f32[2]{0:T(128)S(1)}) all-reduce(f32[2]{0:T(128)S(1)} %get-tuple-element.8, f32[2]{0:T(128)S(1)} %get-tuple-element.7), channel_id=1, replica_groups=mesh['gx'=16,'gy'=4,'gz'=8] {'gy','gz'}, use_global_device_ids=true, to_apply=%region_7.8 | all-reduce | flops 4 | bytes 32 | tf_op jit(solution)/shard_map/psum | solution.py:88
  350.8 77.0 %all-reduce.9 = (f32[2]{0:T(128)S(1)}, f32[2]{0:T(128)S(1)}) all-reduce(f32[2]{0:T(128)S(1)} %get-tuple-element.21, f32[2]{0:T(128)S(1)} %get-tuple-element.22), channel_id=1, replica_groups=mesh['gx'=16,'gy'=4,'gz'=8] {'gx'}, use_global_device_ids=true, to_apply=%region_8.9 | all-reduce | flops 4 | bytes 32 | tf_op jit(solution)/shard_map/psum | solution.py:88
  430.4 3.9 collective-permute-start.13
  436.6 4.0 collective-permute-start.15
  443.0 4.0 collective-permute-start.17
  449.7 101.4 %all-reduce.4 = (f32[2]{0:T(128)S(1)}, f32[2]{0:T(128)S(1)}) all-reduce(f32[2]{0:T(128)S(1)} %get-tuple-element.6, f32[2]{0:T(128)S(1)} %get-tuple-element.5), channel_id=1, replica_groups=mesh['gx'=16,'gy'=4,'gz'=8] {'gy','gz'}, use_global_device_ids=true, to_apply=%region_13.14 | all-reduce | flops 4 | bytes 32 | tf_op jit(solution)/shard_map/psum | solution.py:88
  551.1 80.9 %all-reduce.8 = (f32[2]{0:T(128)S(1)}, f32[2]{0:T(128)S(1)}) all-reduce(f32[2]{0:T(128)S(1)} %get-tuple-element.19, f32[2]{0:T(128)S(1)} %get-tuple-element.20), channel_id=1, replica_groups=mesh['gx'=16,'gy'=4,'gz'=8] {'gx'}, use_global_device_ids=true, to_apply=%region_14.15 | all-reduce | flops 4 | bytes 32 | tf_op jit(solution)/shard_map/psum | solution.py:88
  634.2 12.2 %collective-permute-start.19 = (bf16[2,1,4,8,192]{4,3,2,1,0:T(8,128)(2,1)S(1)}, bf16[2,1,4,8,192]{4,3,2,1,0:T(8,128)(2,1)S(1)}, u32[]{:S(2)}, u32[]{:S(2)}) collective-permute-start(bf16[2,1,4,8,192]{4,3,2,1,0:T(8,128)(2,1)S(1)} %get-tuple-element.84), channel_id=1, source_target_pairs={{0,32},{32,64},{64,96},{96,128},{128,160},{160,192},{192,224},{224... | collective-permute-start | bytes 73736 | tf_op jit(solution)/shard_map/ppermute | solution.py:17
  648.8 4.0 collective-permute-start.21
  655.2 4.0 collective-permute-start.23
  661.8 101.8 %all-reduce.3 = (f32[2]{0:T(128)S(1)}, f32[2]{0:T(128)S(1)}) all-reduce(f32[2]{0:T(128)S(1)} %get-tuple-element.4, f32[2]{0:T(128)S(1)} %get-tuple-element.3), channel_id=1, replica_groups=mesh['gx'=16,'gy'=4,'gz'=8] {'gy','gz'}, use_global_device_ids=true, to_apply=%region_19.20 | all-reduce | flops 4 | bytes 32 | tf_op jit(solution)/shard_map/psum | solution.py:88
  763.6 80.6 %all-reduce.7 = (f32[2]{0:T(128)S(1)}, f32[2]{0:T(128)S(1)}) all-reduce(f32[2]{0:T(128)S(1)} %get-tuple-element.17, f32[2]{0:T(128)S(1)} %get-tuple-element.18), channel_id=1, replica_groups=mesh['gx'=16,'gy'=4,'gz'=8] {'gx'}, use_global_device_ids=true, to_apply=%region_20.21 | all-reduce | flops 4 | bytes 32 | tf_op jit(solution)/shard_map/psum | solution.py:88
  846.0 136.9 %all-reduce.2 = (f32[4096]{0:T(1024)S(1)}, f32[4096]{0:T(1024)S(1)}) all-reduce(f32[4096]{0:T(1024)S(1)} %scatter_custom_fusion.1, f32[4096]{0:T(1024)S(1)} %scatter_custom_fusion), channel_id=3, replica_groups=mesh['gx'=16,'gy'=4,'gz'=8] {'gx','gy','gz'}, use_global_device_ids=true, to_apply=%region_28.29.clone | all-reduce | flops 8192 | bytes 65536
  (127 shorter events, 39.9 us)
Async XLA Ops:
  15.3 10.8 %collective-permute-start = (bf16[2,1,4,8,192]{4,3,2,1,0:T(8,128)(2,1)S(1)}, bf16[2,1,4,8,192]{4,3,2,1,0:T(8,128)(2,1)S(1)}, u32[]{:S(2)}, u32[]{:S(2)}) collective-permute-start(bf16[2,1,4,8,192]{4,3,2,1,0:T(8,128)(2,1)S(1)} %get-tuple-element.91), channel_id=1, source_target_pairs={{32,0},{64,32},{96,64},{128,96},{160,128},{192,160},{224,192},{256... | collective-permute-start | bytes 73736 | tf_op jit(solution)/shard_map/ppermute | solution.py:18
  24.1 3.1 collective-permute-start.1
  27.2 5.6 collective-permute-start.2
  28.5 5.0 collective-permute-start.3
  33.6 6.0 collective-permute-start.4
  34.9 5.2 collective-permute-start.5
  228.4 5.6 collective-permute-start.6
  230.9 4.0 collective-permute-start.7
  235.0 5.6 collective-permute-start.8
  236.3 5.2 collective-permute-start.9
  241.5 6.0 collective-permute-start.10
  242.8 5.2 collective-permute-start.11
  427.9 6.5 collective-permute-start.12
  430.4 4.9 collective-permute-start.13
  435.3 5.6 collective-permute-start.14
  436.6 5.0 collective-permute-start.15
  441.7 6.0 collective-permute-start.16
  443.0 5.3 collective-permute-start.17
  632.1 15.4 %collective-permute-start.18 = (bf16[2,1,4,8,192]{4,3,2,1,0:T(8,128)(2,1)S(1)}, bf16[2,1,4,8,192]{4,3,2,1,0:T(8,128)(2,1)S(1)}, u32[]{:S(2)}, u32[]{:S(2)}) collective-permute-start(bf16[2,1,4,8,192]{4,3,2,1,0:T(8,128)(2,1)S(1)} %get-tuple-element.85), channel_id=1, source_target_pairs={{32,0},{64,32},{96,64},{128,96},{160,128},{192,160},{224,192},{256... | collective-permute-start | bytes 73736 | tf_op jit(solution)/shard_map/ppermute | solution.py:18
  634.2 13.3 %collective-permute-start.19 = (bf16[2,1,4,8,192]{4,3,2,1,0:T(8,128)(2,1)S(1)}, bf16[2,1,4,8,192]{4,3,2,1,0:T(8,128)(2,1)S(1)}, u32[]{:S(2)}, u32[]{:S(2)}) collective-permute-start(bf16[2,1,4,8,192]{4,3,2,1,0:T(8,128)(2,1)S(1)} %get-tuple-element.84), channel_id=1, source_target_pairs={{0,32},{32,64},{64,96},{96,128},{128,160},{160,192},{192,224},{224... | collective-permute-start | bytes 73736 | tf_op jit(solution)/shard_map/ppermute | solution.py:17
  647.5 5.6 collective-permute-start.20
  648.8 5.0 collective-permute-start.21
  653.9 6.0 collective-permute-start.22
  655.2 5.2 collective-permute-start.23
  (7 other events, 908.2 us)
